TPU v7x, 256 devices: a whole 4x4x8 slice. The times are simulated.
256 devices in a mesh: gx: 8 (over z), gy: 32 (over x, y, core).
Axes of the slice: x: 4, y: 4, z: 8, core: 2. Of those that a mesh axis runs over, the one named last changes fastest.
Arguments:
- permeability: float32 [3, 256, 65536], P(None, 'gx', 'gy'), may hold values from 0.03 to 1000, as said below
Outputs:
- fine_pressure: float32 [256, 65536], P('gx', 'gy')
- twin_pressure: float32 [128, 16384], P('gx', 'gy')
Inputs may be any that keep to these rules, and one draw needn't show every extreme that they name: `permeability`: positive conductivities; entry 0, 1, 2 of the first dimension is the conductivity along the grid's first, second, third dimension.
All inputs are finite; a program needn't handle non-finite values.
Results may differ from a plain program's by a relative error of at most 0.0003.
Values sent between devices are 32-bit elements; how exact they have to be, the bound alone decides.
A program may use at most 192 MiB of HBM per device.

v0:
```python
import jax
import jax.numpy as jnp
from jax import lax
from jax.sharding import PartitionSpec as P

EL = 32
ELZ = 16
MX = 4
MZ = 2
EZ = 2
PATCH_ITERS = 3
COARSE_ITERS = 2


def shifted(shard, axis, by):
    count = lax.axis_size(axis)
    return lax.ppermute(shard, axis, [(i, (i + by) % count) for i in range(count)])


def padded_2(cells, sides, width):
    for axis, dim in sides:
        count = lax.axis_size(axis)
        head = lax.slice_in_dim(cells, 0, width, axis=dim)
        tail = lax.slice_in_dim(cells, cells.shape[dim] - width, cells.shape[dim], axis=dim)
        cells = jnp.concatenate(
            [
                lax.ppermute(tail, axis, [(i, (i + 1) % count) for i in range(count)]),
                cells,
                lax.ppermute(head, axis, [((i + 1) % count, i) for i in range(count)]),
            ],
            axis=dim,
        )
    return cells


def harmonic(first, second, spacing):
    return spacing * 2.0 * first * second / (first + second)


def face_weights(conduct, width, spacing):
    weight_rows = harmonic(conduct[0][..., :-width], conduct[0][..., width:], spacing)
    weight_cols = harmonic(conduct[1][..., :-1], conduct[1][..., 1:], spacing)
    column = jnp.arange(weight_cols.shape[-1], dtype=jnp.int32) % width
    weight_cols = jnp.where(column == width - 1, jnp.zeros_like(weight_cols), weight_cols)
    weight_depth = harmonic(conduct[2][:, :-1], conduct[2][:, 1:], spacing)
    return (weight_rows, weight_cols, weight_depth)


def apply_operator(field, weights, width):
    weight_rows, weight_cols, weight_depth = weights
    flux = weight_rows * (field[..., :-width] - field[..., width:])
    result = jnp.pad(flux, ((0, 0), (0, 0), (0, 0), (0, width))) - jnp.pad(
        flux, ((0, 0), (0, 0), (0, 0), (width, 0))
    )
    flux = weight_cols * (field[..., :-1] - field[..., 1:])
    result = (
        result
        + jnp.pad(flux, ((0, 0), (0, 0), (0, 0), (0, 1)))
        - jnp.pad(flux, ((0, 0), (0, 0), (0, 0), (1, 0)))
    )
    flux = weight_depth * (field[:, :, :-1] - field[:, :, 1:])
    result = (
        result
        + jnp.pad(flux, ((0, 0), (0, 0), (0, 1), (0, 0)))
        - jnp.pad(flux, ((0, 0), (0, 0), (1, 0), (0, 0)))
    )
    return result


def interior_mask(depth, rows, width):
    level = jnp.arange(depth, dtype=jnp.int32)[:, None]
    cell = jnp.arange(rows * width, dtype=jnp.int32)[None, :]
    row_index = cell // width
    line_index = cell % width
    inside = (
        (level > 0)
        & (level < depth - 1)
        & (row_index > 0)
        & (row_index < rows - 1)
        & (line_index > 0)
        & (line_index < width - 1)
    )
    return inside.astype(jnp.float32)


def shape_functions(depth, rows, width, edge, edge_depth, margin, margin_depth):
    cell = jnp.arange(rows * width, dtype=jnp.int32)
    place_rows = ((cell // width).astype(jnp.float32) - margin + 0.5) / edge
    place_cols = ((cell % width).astype(jnp.float32) - margin + 0.5) / edge
    place_depth = (
        jnp.arange(depth, dtype=jnp.int32).astype(jnp.float32) - margin_depth + 0.5
    ) / edge_depth
    factors = []
    for basis in range(8):
        along_rows = place_rows if basis // 4 else 1.0 - place_rows
        along_cols = place_cols if basis // 2 % 2 else 1.0 - place_cols
        along_depth = place_depth if basis % 2 else 1.0 - place_depth
        factors.append(along_depth[:, None] * (along_rows * along_cols)[None, :])
    return jnp.stack(factors)[:, None]


def patch_fields(block, edge_depth, margin_depth):
    depth = edge_depth + 2 * margin_depth
    count = (block.shape[3] - 2 * margin_depth) // edge_depth
    pieces = [
        block[:, :, :, index * edge_depth : index * edge_depth + depth] for index in range(count)
    ]
    stacked = jnp.stack(pieces, axis=1)
    return jnp.transpose(stacked, (0, 1, 4, 2, 3)).reshape(
        3, count, depth, block.shape[1] * block.shape[2]
    )


def solve_column(block, edge, edge_depth, margin, margin_depth, spacing):
    rows = block.shape[1]
    width = block.shape[2]
    depth = edge_depth + 2 * margin_depth
    conduct = patch_fields(block, edge_depth, margin_depth)
    count = conduct.shape[1]
    weights = face_weights(conduct, width, spacing)
    inside = interior_mask(depth, rows, width)
    start = shape_functions(depth, rows, width, edge, edge_depth, margin, margin_depth)
    residual = -inside * apply_operator(start, weights, width)
    direction = residual
    norm_now = jnp.sum(residual * residual, axis=(2, 3), keepdims=True)
    update = jnp.zeros_like(residual)
    for step in range(PATCH_ITERS):
        image = inside * apply_operator(direction, weights, width)
        alpha = norm_now / jnp.sum(direction * image, axis=(2, 3), keepdims=True)
        update = update + alpha * direction
        residual = residual - alpha * image
        norm_next = jnp.sum(residual * residual, axis=(2, 3), keepdims=True)
        direction = residual + norm_next / norm_now * direction
        norm_now = norm_next
    solution = start + update
    local = solution.reshape(8, count, depth, rows, width)[
        :,
        :,
        margin_depth : margin_depth + edge_depth,
        margin : margin + edge,
        margin : margin + edge,
    ]
    local = local.reshape(8, count, edge_depth, edge * edge)
    element_conduct = conduct.reshape(3, count, depth, rows, width)[
        :,
        :,
        margin_depth : margin_depth + edge_depth,
        margin : margin + edge,
        margin : margin + edge,
    ]
    element_conduct = element_conduct.reshape(3, count, edge_depth, edge * edge)
    inner_rows, inner_cols, inner_depth = face_weights(element_conduct, edge, spacing)
    jump = local[..., :-edge] - local[..., edge:]
    stiffness = jnp.einsum(
        "aezn,bezn->eab", jump * inner_rows, jump, precision=lax.Precision.HIGHEST
    )
    jump = local[..., :-1] - local[..., 1:]
    stiffness = stiffness + jnp.einsum(
        "aezn,bezn->eab", jump * inner_cols, jump, precision=lax.Precision.HIGHEST
    )
    jump = local[:, :, :-1] - local[:, :, 1:]
    stiffness = stiffness + jnp.einsum(
        "aezn,bezn->eab", jump * inner_depth, jump, precision=lax.Precision.HIGHEST
    )
    return (local, stiffness)


def coarsen(block):
    comps, rows, width, depth = block.shape
    grouped = block.reshape(comps, rows // 2, 2, width // 2, 2, depth // 2, 2)
    return 0.125 * jnp.sum(grouped, axis=(2, 4, 6))


def corner_stack(corner_first, corner_rows, corner_cols, corner_both, count):
    table = [[corner_first, corner_cols], [corner_rows, corner_both]]
    values = []
    for basis in range(8):
        lift = basis % 2
        values.append(table[basis // 4][basis // 2 % 2][..., lift : lift + count])
    return jnp.stack(values, axis=-1)


def spread(values):
    parts = [[None, None], [None, None]]
    for basis in range(8):
        lift = basis % 2
        widths = [(0, 0)] * (values.ndim - 2) + [(lift, 1 - lift)]
        padded = jnp.pad(values[..., basis], widths)
        first = basis // 4
        second = basis // 2 % 2
        if parts[first][second] is None:
            parts[first][second] = padded
        else:
            parts[first][second] = parts[first][second] + padded
    return parts


def pressure_tile(local, weights, edge):
    combined = jnp.sum(jnp.transpose(weights)[:, :, None, None] * local, axis=0)
    count = combined.shape[0]
    depth = combined.shape[1]
    return jnp.transpose(combined.reshape(count, depth, edge, edge), (2, 3, 0, 1)).reshape(
        edge, edge, count * depth
    )


def neighbours(nodes):
    next_rows = shifted(nodes, "gx", -1)
    fetched = shifted(jnp.stack([nodes[:, 0], next_rows[:, 0]]), "gy", -1)
    next_cols = jnp.concatenate([nodes[:, 1:], fetched[0][:, None]], axis=1)
    next_both = jnp.concatenate([next_rows[:, 1:], fetched[1][:, None]], axis=1)
    return (next_rows, next_cols, next_both)


def local_operator(stiffness, nodes, count):
    next_rows, next_cols, next_both = neighbours(nodes)
    element = corner_stack(nodes, next_rows, next_cols, next_both, count)
    local = jnp.einsum("lckab,lckb->lcka", stiffness, element, precision=lax.Precision.HIGHEST)
    parts = spread(local)
    col_part = parts[0][1]
    both_part = parts[1][1]
    returned = shifted(jnp.stack([col_part[:, -1], both_part[:, -1]]), "gy", 1)
    moved_cols = jnp.concatenate([returned[0][:, None], col_part[:, :-1]], axis=1)
    moved_both = jnp.concatenate([returned[1][:, None], both_part[:, :-1]], axis=1)
    across = shifted(parts[1][0] + moved_both, "gx", 1)
    return parts[0][0] + moved_cols + across


def squares(residual):
    return lax.psum(jnp.sum(residual * residual, axis=(1, 2), keepdims=True), ("gx", "gy"))


def spread_solve(stiffness, columns, count):
    level = jnp.arange(count + 1, dtype=jnp.int32)
    inside = ((level > 0) & (level < count)).astype(jnp.float32)
    boundary = jnp.broadcast_to((level == 0).astype(jnp.float32), (2, columns, count + 1))
    source = -inside * local_operator(stiffness, boundary, count)
    update = jnp.zeros_like(source)
    residual = source
    direction = source
    norm_now = squares(residual)
    for step in range(COARSE_ITERS):
        image = inside * local_operator(stiffness, direction, count)
        alpha = norm_now / lax.psum(
            jnp.sum(direction * image, axis=(1, 2), keepdims=True), ("gx", "gy")
        )
        update = update + alpha * direction
        residual = residual - alpha * image
        norm_next = squares(residual)
        direction = residual + norm_next / norm_now * direction
        norm_now = norm_next
    return boundary + update


def shards(permeability):
    depth_total = ELZ * EZ
    shaped = permeability.reshape(
        3, permeability.shape[1], permeability.shape[2] // depth_total, depth_total
    )
    rimmed = padded_2(shaped, (("gx", 1), ("gy", 2)), MX)
    half_edge = EL // 2
    columns = shaped.shape[2] // EL

    def column_work(offset):
        block = lax.dynamic_slice_in_dim(rimmed, offset, EL + 2 * MX, 2)
        fine_block = jnp.pad(block, ((0, 0), (0, 0), (0, 0), (MZ, MZ)), mode="edge")
        twin_block = coarsen(fine_block)
        fine_local, fine_stiff = solve_column(fine_block, EL, ELZ, MX, MZ, 1.0)
        twin_local, twin_stiff = solve_column(
            twin_block, half_edge, ELZ // 2, MX // 2, MZ // 2, 2.0
        )
        return (fine_local, fine_stiff, twin_local, twin_stiff)

    offsets = jnp.arange(columns, dtype=jnp.int32) * EL
    fine_local, fine_stiff, twin_local, twin_stiff = lax.map(column_work, offsets)
    stiffness = jnp.stack([fine_stiff, twin_stiff])
    count = stiffness.shape[2]
    corner_first = spread_solve(stiffness, columns, count)
    corner_rows, corner_cols, corner_both = neighbours(corner_first)
    weights = corner_stack(corner_first, corner_rows, corner_cols, corner_both, count)
    fine_tiles = [
        pressure_tile(fine_local[column], weights[0, column], EL) for column in range(columns)
    ]
    twin_tiles = [
        pressure_tile(twin_local[column], weights[1, column], half_edge)
        for column in range(columns)
    ]
    fine_pressure = jnp.concatenate(fine_tiles, axis=1)
    twin_pressure = jnp.concatenate(twin_tiles, axis=1)
    return (fine_pressure.reshape(EL, -1), twin_pressure.reshape(half_edge, -1))


def solution(mesh):
    placed = (P(None, "gx", "gy"),)
    return jax.shard_map(
        shards,
        mesh=mesh,
        in_specs=placed,
        out_specs=(P("gx", "gy"), P("gx", "gy")),
        check_vma=False,
    )
```

profile of v0, /device:TPU:1, one launch (start us, length us, event | category | flops | bytes accessed | tf_op | source)
XLA Modules:
  0.0 635.2 jit_solution(149568154038995864)
XLA Ops:
  0.6 2.1 reshape.1460
  3.7 2.5 collective-permute-start
  6.1 3.9 collective-permute-start.1
  13.8 4.4 collective-permute-done.4
  21.2 2.5 collective-permute-done.5
  25.7 1.9 copy-done.12
  27.6 2.6 collective-permute-start.3
  32.8 2.7 copy.335
  35.6 2.1 copy.336
  37.6 2.0 copy.334
  39.7 4.5 pad_maximum_fusion.3
  44.2 299.3 %while.21 = (s32[]{:T(128)}, f32[2,8,2,16,1024]{4,1,3,2,0:T(8,128)}, f32[2,2,8,8]{3,2,1,0:T(8,128)}, f32[2,8,2,8,256]{4,1,3,2,0:T(8,128)}, f32[2,2,8,8]{3,2,1,0:...) while((s32[]{:T(128)}, ...), condition=%wide.region_14.15_spmd, body=%wide.region_0.14_spmd.sunk | while | flops 130577320 | bytes 255059728 | solution.py:275
  45.1 1.7 stack.282
  50.3 2.1 constant_dynamic-slice_fusion.2
  62.3 2.2 reshape.1501
  66.1 1.6 broadcast_multiply_fusion.34
  69.1 2.2 reshape.1502
  88.3 2.0 add_add_fusion.5
  90.3 5.9 reshape.1503
  96.2 5.7 slice.2293
  102.0 3.7 broadcast_in_dim.249
  106.8 3.9 reshape.1504
  110.7 2.9 fusion.260
  113.6 1.9 squeeze.279
  116.6 2.3 fusion.261
  118.9 1.9 squeeze.280
  121.9 2.5 fusion.262
  126.4 3.0 fusion.264
  131.4 26.2 %reshape.1505 = f32[3,20,2,20,2,18,2]{4,3,2,1,6,5,0:T(8,128)} reshape(f32[3,40,40,36]{2,1,3,0:T(8,128)} %pad_maximum_fusion.26) | data formatting | bytes 1382400 | tf_op jit(solution)/shard_map/while/body/eval_jaxpr/reshape | solution.py:170
  157.7 19.5 %reduce_sum.329 = f32[3,20,20,18]{2,1,3,0:T(8,128)S(1)} reduce(f32[3,20,2,20,2,18,2]{4,3,2,1,6,5,0:T(8,128)} %reshape.1505, f32[]{:T(128)} %constant.340.clone.31..sunk), dimensions={2,4,6}, to_apply=%region_7.7 | reduce | flops 151200 | bytes 777604 | tf_op jit(solution)/shard_map/while/body/eval_jaxpr/reduce_sum | solution.py:171
  182.1 1.9 reshape.1506
  184.0 1.8 slice.2294
  190.5 1.7 stack.282
  195.8 2.1 constant_dynamic-slice_fusion.2
  207.8 2.2 reshape.1501
  214.6 2.2 reshape.1502
  233.5 2.0 add_add_fusion.5
  235.5 5.9 reshape.1503
  241.5 5.7 slice.2293
  247.2 3.7 broadcast_in_dim.249
  252.0 4.0 reshape.1504
  256.0 2.9 fusion.260
  258.9 1.9 squeeze.279
  261.8 2.3 fusion.261
  264.1 1.9 squeeze.280
  267.2 2.5 fusion.262
  271.7 3.0 fusion.264
  276.7 26.2 %reshape.1505 = f32[3,20,2,20,2,18,2]{4,3,2,1,6,5,0:T(8,128)} reshape(f32[3,40,40,36]{2,1,3,0:T(8,128)} %pad_maximum_fusion.26) | data formatting | bytes 1382400 | tf_op jit(solution)/shard_map/while/body/eval_jaxpr/reshape | solution.py:170
  302.9 19.7 %reduce_sum.329 = f32[3,20,20,18]{2,1,3,0:T(8,128)S(1)} reduce(f32[3,20,2,20,2,18,2]{4,3,2,1,6,5,0:T(8,128)} %reshape.1505, f32[]{:T(128)} %constant.340.clone.31..sunk), dimensions={2,4,6}, to_apply=%region_7.7 | reduce | flops 151200 | bytes 777604 | tf_op jit(solution)/shard_map/while/body/eval_jaxpr/reduce_sum | solution.py:171
  327.6 1.9 reshape.1506
  329.5 1.8 slice.2294
  344.9 7.2 %collective-permute-done.6 = f32[2,2,3]{2,1,0:T(2,128)S(1)} collective-permute-done((f32[2,2,3]{2,1,0:T(2,128)S(1)}, f32[2,2,3]{2,1,0:T(2,128)S(1)}, u32[]{:S(2)}, u32[]{:S(2)}) %collective-permute-start.6) | collective-permute-done | bytes 80 | tf_op jit(solution)/shard_map/ppermute | solution.py:17
  352.2 4.6 collective-permute-done.7
  360.1 7.4 %collective-permute-start.9 = (f32[2,2,3]{2,1,0:T(2,128)S(1)}, f32[2,2,3]{2,1,0:T(2,128)S(1)}, u32[]{:S(2)}, u32[]{:S(2)}) collective-permute-start(f32[2,2,3]{2,1,0:T(2,128)S(1)} %pad_maximum_fusion.20), channel_id=1, source_target_pairs={{0,31},{1,0},{2,1},{3,2},{4,3},{5,4},{6,5},{7,6},{8,7},{9,8},{10,9... | collective-permute-start | bytes 152 | tf_op jit(solution)/shard_map/ppermute | solution.py:17
  371.6 4.2 collective-permute-done.11
  376.6 77.9 %all-reduce.72 = (f32[2,1,1]{0,2,1:T(1,128)S(1)}, f32[2,1,1]{0,2,1:T(1,128)S(1)}) all-reduce(f32[2,1,1]{0,2,1:T(1,128)S(1)} %bitcast.449, f32[2,1,1]{0,2,1:T(1,128)S(1)} %bitcast.448), channel_id=1, replica_groups=mesh['gx'=8,'gy'=32] {'gx','gy'}, use_global_device_ids=true, to_apply=%region_16.17 | all-reduce | flops 4 | bytes 32 | tf_op jit(solution)/shard_map/psum | solution.py:230
  454.7 73.6 %psum.30 = f32[2,1,1]{0,2,1:T(1,128)S(1)} all-reduce(f32[2,1,1]{0,2,1:T(1,128)S(1)} %bitcast.451), channel_id=1, replica_groups=mesh['gx'=8,'gy'=32] {'gx','gy'}, use_global_device_ids=true, to_apply=%region_20.21 | all-reduce | flops 2 | bytes 16 | tf_op jit(solution)/shard_map/psum | solution.py:230
  528.5 1.7 collective-permute-start.12
  533.1 2.0 collective-permute-done.13
  538.3 1.7 collective-permute-start.15
  540.0 2.5 collective-permute-done.15
  543.3 77.1 %psum.31 = f32[2,1,1]{0,2,1:T(1,128)S(1)} all-reduce(f32[2,1,1]{0,2,1:T(1,128)S(1)} %bitcast.450), channel_id=1, replica_groups=mesh['gx'=8,'gy'=32] {'gx','gy'}, use_global_device_ids=true, to_apply=%region_22.23 | all-reduce | flops 2 | bytes 16 | tf_op jit(solution)/shard_map/psum | solution.py:244
  623.9 1.8 collective-permute-start.17
  628.3 2.3 fusion.116
  (519 shorter events, 135.0 us)
Async XLA Ops:
  3.7 20.6 %collective-permute-start = (f32[3,4,64,32]{3,2,1,0:T(8,128)}, f32[3,4,64,32]{3,2,1,0:T(8,128)}, u32[]{:S(2)}, u32[]{:S(2)}) collective-permute-start(f32[3,4,64,32]{3,2,1,0:T(8,128)} %get-tuple-element.370), channel_id=1, source_target_pairs={{0,32},{32,64},{64,96},{96,128},{128,160},{160,192},{192,224},{224... | collective-permute-start | bytes 294920 | tf_op jit(solution)/shard_map/ppermute | solution.py:27
  6.1 19.5 %collective-permute-start.1 = (f32[3,4,64,32]{3,2,1,0:T(8,128)}, f32[3,4,64,32]{3,2,1,0:T(8,128)S(1)}, u32[]{:S(2)}, u32[]{:S(2)}) collective-permute-start(f32[3,4,64,32]{3,2,1,0:T(8,128)} %get-tuple-element.369), channel_id=1, source_target_pairs={{32,0},{64,32},{96,64},{128,96},{160,128},{192,160},{224,192},{0,2... | collective-permute-start | bytes 294920 | tf_op jit(solution)/shard_map/ppermute | solution.py:29
  10.1 20.1 %copy-start.18 = (f32[3]{0:T(128)}, f32[3]{0:T(128)S(1)}, u32[]{:S(2)}) copy-start(f32[3]{0:T(128)S(1)} %compare_convert_fusion) | copy-start | bytes 40
  10.1 8.1 %collective-permute-start.4 = (f32[2,2,3]{2,0,1:T(2,128)S(1)}, f32[2,2,3]{2,0,1:T(2,128)S(1)}, u32[]{:S(2)}, u32[]{:S(2)}) collective-permute-start(f32[2,2,3]{2,0,1:T(2,128)S(1)} %broadcast_in_dim.227), channel_id=1, source_target_pairs={{0,224},{32,0},{64,32},{96,64},{128,96},{160,128},{192,160},{224,1... | collective-permute-start | bytes 152 | tf_op jit(solution)/shard_map/ppermute | solution.py:17
  19.3 4.3 collective-permute-start.5
  25.4 4.9 copy-start.19
  25.6 1.9 copy-start.12
  27.6 7.9 %collective-permute-start.3 = (f32[3,40,4,32]{3,2,1,0:T(4,128)S(1)}, f32[3,40,4,32]{3,2,1,0:T(4,128)S(1)}, u32[]{:S(2)}, u32[]{:S(2)}) collective-permute-start(f32[3,40,4,32]{3,2,1,0:T(4,128)S(1)} %get-tuple-element.368), channel_id=1, source_target_pairs={{1,0},{2,1},{3,2},{4,3},{5,4},{6,5},{7,6},{8,7},{9,8},{10,9},{11,1... | collective-permute-start | bytes 184328 | tf_op jit(solution)/shard_map/ppermute | solution.py:29
  30.2 7.4 %collective-permute-start.2 = (f32[3,40,4,32]{3,2,1,0:T(4,128)S(1)}, f32[3,40,4,32]{3,2,1,0:T(4,128)S(1)}, u32[]{:S(2)}, u32[]{:S(2)}) collective-permute-start(f32[3,40,4,32]{3,2,1,0:T(4,128)S(1)} %get-tuple-element.367), channel_id=1, source_target_pairs={{0,1},{1,2},{2,3},{3,4},{4,5},{5,6},{6,7},{7,8},{8,9},{9,10},{10,1... | collective-permute-start | bytes 184328 | tf_op jit(solution)/shard_map/ppermute | solution.py:27
  39.7 4.5 copy-start.20
  53.6 0.6 copy-start.8
  53.7 0.7 copy-start.10
  54.5 2.3 copy-start
  58.3 1.2 copy-start.7
  64.5 1.6 copy-start.5
  66.1 3.0 copy-start.3
  71.3 1.6 copy-start.6
  72.8 1.6 copy-start.1
  72.8 2.2 copy-start.2
  76.3 1.0 copy-start.4
  125.3 4.6 copy-start.9
  125.3 4.6 copy-start.11
  184.0 2.2 copy-start.13
  185.8 2.6 copy-start.16
  186.3 3.2 copy-start.21
  186.3 2.6 copy-start.14
  188.9 0.6 copy-start.17
  199.1 0.6 copy-start.8
  199.1 0.7 copy-start.10
  199.9 2.3 copy-start
  203.7 1.2 copy-start.7
  210.0 1.6 copy-start.5
  211.6 3.0 copy-start.3
  216.7 1.6 copy-start.6
  218.3 1.6 copy-start.1
  218.3 2.2 copy-start.2
  221.8 1.0 copy-start.4
  270.5 4.6 copy-start.9
  270.5 4.6 copy-start.11
  329.5 2.2 copy-start.13
  331.3 2.6 copy-start.16
  331.8 3.2 copy-start.21
  331.8 2.6 copy-start.14
  334.3 0.6 copy-start.17
  344.8 7.3 %collective-permute-start.6 = (f32[2,2,3]{2,1,0:T(2,128)S(1)}, f32[2,2,3]{2,1,0:T(2,128)S(1)}, u32[]{:S(2)}, u32[]{:S(2)}) collective-permute-start(f32[2,2,3]{2,1,0:T(2,128)S(1)} %pad_maximum_fusion.19), channel_id=1, source_target_pairs={{0,1},{1,2},{2,3},{3,4},{4,5},{5,6},{6,7},{7,8},{8,9},{9,10},{10,1... | collective-permute-start | bytes 152 | tf_op jit(solution)/shard_map/ppermute | solution.py:17
  352.2 4.6 collective-permute-start.7
  357.6 2.4 collective-permute-start.8
  360.1 8.2 %collective-permute-start.9 = (f32[2,2,3]{2,1,0:T(2,128)S(1)}, f32[2,2,3]{2,1,0:T(2,128)S(1)}, u32[]{:S(2)}, u32[]{:S(2)}) collective-permute-start(f32[2,2,3]{2,1,0:T(2,128)S(1)} %pad_maximum_fusion.20), channel_id=1, source_target_pairs={{0,31},{1,0},{2,1},{3,2},{4,3},{5,4},{6,5},{7,6},{8,7},{9,8},{10,9... | collective-permute-start | bytes 152 | tf_op jit(solution)/shard_map/ppermute | solution.py:17
  370.2 1.2 collective-permute-start.10
  371.5 4.2 collective-permute-start.11
  528.5 2.7 collective-permute-start.12
  531.2 3.9 collective-permute-start.13
  537.0 1.2 collective-permute-start.14
  538.3 4.2 collective-permute-start.15
  621.2 2.7 collective-permute-start.16
  623.9 3.7 collective-permute-start.17
  631.5 1.8 copy-start.15
where the time goes:
time: 646 us; the launch traced here: 635 us
  blocking collectives  229 us (35%)
  local copies, waits for them, and re-layouts  188 us (29%)
  other arithmetic  118 us (18%)
  waiting for transfers between devices  34.7 us (5%)
  starting transfers between devices  28.8 us (4%)
  matrix products  20.8 us (3%)
  loops' own time  14.6 us (2%)
    psum x2, blocking collectives, squares(): lax.psum(jnp.sum(residual * residual, axis=(1, 2), keepdims=True), ('gx',...  152 us
    psum x1, blocking collectives, spread_solve(): lax.psum(jnp.sum(direction * image, axis=(1, 2), keepdims=True), ('gx', '...  77.1 us
    reshape x2, local copies, waits for them, and re-layouts, coarsen(): grouped = block.reshape(comps, rows // 2, 2, width // 2, 2, depth // 2, 2)  52.5 us
    reduce_sum x2, other arithmetic, coarsen(): return 0.125 * jnp.sum(grouped, axis=(2, 4, 6))  39.3 us
    ppermute x14, waiting for transfers between devices, shifted(): lax.ppermute(shard, axis, [(i, (i + by) % count) for i in range(count)])  34.7 us
    ppermute x14, starting transfers between devices, shifted(): lax.ppermute(shard, axis, [(i, (i + by) % count) for i in range(count)])  19.8 us
    reshape x4, local copies, waits for them, and re-layouts, solve_column(): solution.reshape(8, count, depth, rows, width)  15.7 us
    slice x4, local copies, waits for them, and re-layouts, solve_column(): solution.reshape(8, count, depth, rows, width)  15 us
  transfers between devices with their start and end apart: 18, of which 14 were waited for; matrix products, arithmetic and copies ran while one was open for 2% of the time, Pallas kernels for 0%

commit v1 on v0

--- a/solution.py
+++ b/solution.py
@@ -241,8 +241,9 @@
     norm_now = squares(residual)
     for step in range(COARSE_ITERS):
         image = inside * local_operator(stiffness, direction, count)
-        alpha = norm_now / lax.psum(
-            jnp.sum(direction * image, axis=(1, 2), keepdims=True), ("gx", "gy")
+        alpha = norm_now / jnp.sum(
+            lax.all_gather(jnp.sum(direction * image, axis=(1, 2), keepdims=True), ("gx", "gy")),
+            axis=0,
         )
         update = update + alpha * direction
         residual = residual - alpha * image

time: 646 us -> 646 us (level)
    unnamed x0 -> x1, blocking collectives: none -> 77.3 us
    psum x1 -> x0, blocking collectives: 77.1 us -> none  [spread_solve(): lax.psum(jnp.sum(direction * image, axis=(1, 2), keepdims=True), ('gx', '...]
where the time goes in v1:
time: 646 us; the launch traced here: 635 us
  blocking collectives  229 us (35%)
  local copies, waits for them, and re-layouts  188 us (29%)
  other arithmetic  119 us (18%)
  waiting for transfers between devices  34.4 us (5%)
  starting transfers between devices  28.7 us (4%)
  matrix products  20.8 us (3%)
  loops' own time  14.1 us (2%)
    psum x2, blocking collectives, squares(): lax.psum(jnp.sum(residual * residual, axis=(1, 2), keepdims=True), ('gx',...  151 us
    unnamed x1, blocking collectives  77.3 us
    reshape x2, local copies, waits for them, and re-layouts, coarsen(): grouped = block.reshape(comps, rows // 2, 2, width // 2, 2, depth // 2, 2)  52.3 us
    reduce_sum x2, other arithmetic, coarsen(): return 0.125 * jnp.sum(grouped, axis=(2, 4, 6))  39.3 us
    ppermute x14, waiting for transfers between devices, shifted(): lax.ppermute(shard, axis, [(i, (i + by) % count) for i in range(count)])  34.4 us
    ppermute x14, starting transfers between devices, shifted(): lax.ppermute(shard, axis, [(i, (i + by) % count) for i in range(count)])  19.6 us
    reshape x4, local copies, waits for them, and re-layouts, solve_column(): solution.reshape(8, count, depth, rows, width)  15.6 us
    slice x4, local copies, waits for them, and re-layouts, solve_column(): solution.reshape(8, count, depth, rows, width)  15 us
  transfers between devices with their start and end apart: 18, of which 14 were waited for; matrix products, arithmetic and copies ran while one was open for 2% of the time, Pallas kernels for 0%

profile of v1, /device:TPU:1, one launch (start us, length us, event | category | flops | bytes accessed | tf_op | source)
XLA Modules:
  0.0 635.0 jit_solution(5073341999664808553)
XLA Ops:
  0.6 2.1 reshape.1462
  3.7 2.5 collective-permute-start
  6.1 3.9 collective-permute-start.1
  13.7 4.5 collective-permute-done.4
  21.1 2.3 collective-permute-done.5
  25.4 1.9 copy-done.12
  27.4 2.8 collective-permute-start.3
  32.7 2.7 copy.335
  35.4 2.1 copy.336
  37.5 2.0 copy.334
  39.6 4.5 pad_maximum_fusion.3
  44.1 298.6 %while.21 = (s32[]{:T(128)}, f32[2,8,2,16,1024]{4,1,3,2,0:T(8,128)}, f32[2,2,8,8]{3,2,1,0:T(8,128)}, f32[2,8,2,8,256]{4,1,3,2,0:T(8,128)}, f32[2,2,8,8]{3,2,1,0:...) while((s32[]{:T(128)}, ...), condition=%wide.region_14.15_spmd, body=%wide.region_0.14_spmd.sunk | while | flops 130577320 | bytes 255059728 | solution.py:276
  45.0 1.7 stack.282
  50.2 2.1 constant_dynamic-slice_fusion.2
  62.2 2.2 reshape.1511
  66.0 1.6 broadcast_multiply_fusion.34
  69.0 2.2 reshape.1512
  88.2 2.0 add_add_fusion.5
  90.2 5.9 reshape.1513
  96.1 5.7 slice.2293
  101.8 3.7 broadcast_in_dim.241
  106.6 3.9 reshape.1514
  110.6 2.9 fusion.262
  113.5 1.9 squeeze.279
  116.4 2.3 fusion.263
  118.7 1.9 squeeze.280
  121.7 2.5 fusion.264
  126.3 3.0 fusion.266
  131.3 26.2 %reshape.1515 = f32[3,20,2,20,2,18,2]{4,3,2,1,6,5,0:T(8,128)} reshape(f32[3,40,40,36]{2,1,3,0:T(8,128)} %pad_maximum_fusion.26) | data formatting | bytes 1382400 | tf_op jit(solution)/shard_map/while/body/eval_jaxpr/reshape | solution.py:170
  157.5 19.5 %reduce_sum.355 = f32[3,20,20,18]{2,1,3,0:T(8,128)S(1)} reduce(f32[3,20,2,20,2,18,2]{4,3,2,1,6,5,0:T(8,128)} %reshape.1515, f32[]{:T(128)} %constant.353.clone.1..sunk), dimensions={2,4,6}, to_apply=%region_7.7 | reduce | flops 151200 | bytes 777604 | tf_op jit(solution)/shard_map/while/body/eval_jaxpr/reduce_sum | solution.py:171
  182.0 1.9 reshape.1516
  183.9 1.8 slice.2294
  190.4 1.7 stack.282
  195.6 2.1 constant_dynamic-slice_fusion.2
  207.6 2.2 reshape.1511
  214.4 2.2 reshape.1512
  233.3 2.0 add_add_fusion.5
  235.4 5.9 reshape.1513
  241.3 5.7 slice.2293
  247.0 3.7 broadcast_in_dim.241
  251.8 4.0 reshape.1514
  255.8 2.9 fusion.262
  258.7 1.9 squeeze.279
  261.6 2.3 fusion.263
  263.9 1.9 squeeze.280
  267.0 2.5 fusion.264
  271.5 3.0 fusion.266
  276.5 26.2 %reshape.1515 = f32[3,20,2,20,2,18,2]{4,3,2,1,6,5,0:T(8,128)} reshape(f32[3,40,40,36]{2,1,3,0:T(8,128)} %pad_maximum_fusion.26) | data formatting | bytes 1382400 | tf_op jit(solution)/shard_map/while/body/eval_jaxpr/reshape | solution.py:170
  302.7 19.7 %reduce_sum.355 = f32[3,20,20,18]{2,1,3,0:T(8,128)S(1)} reduce(f32[3,20,2,20,2,18,2]{4,3,2,1,6,5,0:T(8,128)} %reshape.1515, f32[]{:T(128)} %constant.353.clone.1..sunk), dimensions={2,4,6}, to_apply=%region_7.7 | reduce | flops 151200 | bytes 777604 | tf_op jit(solution)/shard_map/while/body/eval_jaxpr/reduce_sum | solution.py:171
  327.4 1.9 reshape.1516
  329.3 1.8 slice.2294
  344.1 7.1 %collective-permute-done.6 = f32[2,2,3]{2,1,0:T(2,128)S(1)} collective-permute-done((f32[2,2,3]{2,1,0:T(2,128)S(1)}, f32[2,2,3]{2,1,0:T(2,128)S(1)}, u32[]{:S(2)}, u32[]{:S(2)}) %collective-permute-start.6) | collective-permute-done | bytes 80 | tf_op jit(solution)/shard_map/ppermute | solution.py:17
  351.3 4.6 collective-permute-done.7
  359.1 7.4 %collective-permute-start.9 = (f32[2,2,3]{2,1,0:T(2,128)S(1)}, f32[2,2,3]{2,1,0:T(2,128)S(1)}, u32[]{:S(2)}, u32[]{:S(2)}) collective-permute-start(f32[2,2,3]{2,1,0:T(2,128)S(1)} %pad_maximum_fusion.20), channel_id=1, source_target_pairs={{0,31},{1,0},{2,1},{3,2},{4,3},{5,4},{6,5},{7,6},{8,7},{9,8},{10,9... | collective-permute-start | bytes 152 | tf_op jit(solution)/shard_map/ppermute | solution.py:17
  370.6 4.2 collective-permute-done.11
  375.9 77.9 %all-reduce.74 = (f32[2,1,1]{0,2,1:T(1,128)S(1)}, f32[512]{0:T(512)S(1)}) all-reduce(f32[2,1,1]{0,2,1:T(1,128)S(1)} %bitcast.454, f32[512]{0:T(512)S(1)} %dynamic-update-slice), channel_id=1, replica_groups=mesh['gx'=8,'gy'=32] {'gx','gy'}, use_global_device_ids=true, to_apply=%region_16.17 | all-reduce | flops 514 | bytes 4112 | tf_op jit(solution)/shard_map/psum | solution.py:230
  454.2 73.6 %psum.15 = f32[2,1,1]{0,2,1:T(1,128)S(1)} all-reduce(f32[2,1,1]{0,2,1:T(1,128)S(1)} %bitcast.455), channel_id=1, replica_groups=mesh['gx'=8,'gy'=32] {'gx','gy'}, use_global_device_ids=true, to_apply=%region_20.21 | all-reduce | flops 2 | bytes 16 | tf_op jit(solution)/shard_map/psum | solution.py:230
  527.9 1.7 collective-permute-start.12
  532.5 2.0 collective-permute-done.13
  537.7 1.7 collective-permute-start.15
  539.4 2.5 collective-permute-done.15
  542.9 77.3 %all-reduce.73 = f32[512]{0:T(512)S(1)} all-reduce(f32[512]{0:T(512)S(1)} %dynamic-update-slice.1), channel_id=3, replica_groups=mesh['gx'=8,'gy'=32] {'gx','gy'}, use_global_device_ids=true, to_apply=%add.73 | all-reduce | flops 512 | bytes 4096
  623.7 1.8 collective-permute-start.17
  628.1 2.3 fusion.116
  (527 shorter events, 135.4 us)
Async XLA Ops:
  3.7 20.4 %collective-permute-start = (f32[3,4,64,32]{3,2,1,0:T(8,128)}, f32[3,4,64,32]{3,2,1,0:T(8,128)}, u32[]{:S(2)}, u32[]{:S(2)}) collective-permute-start(f32[3,4,64,32]{3,2,1,0:T(8,128)} %get-tuple-element.370), channel_id=1, source_target_pairs={{0,32},{32,64},{64,96},{96,128},{128,160},{160,192},{192,224},{224... | collective-permute-start | bytes 294920 | tf_op jit(solution)/shard_map/ppermute | solution.py:27
  6.1 19.2 %collective-permute-start.1 = (f32[3,4,64,32]{3,2,1,0:T(8,128)}, f32[3,4,64,32]{3,2,1,0:T(8,128)S(1)}, u32[]{:S(2)}, u32[]{:S(2)}) collective-permute-start(f32[3,4,64,32]{3,2,1,0:T(8,128)} %get-tuple-element.369), channel_id=1, source_target_pairs={{32,0},{64,32},{96,64},{128,96},{160,128},{192,160},{224,192},{0,2... | collective-permute-start | bytes 294920 | tf_op jit(solution)/shard_map/ppermute | solution.py:29
  10.1 20.0 %copy-start.18 = (f32[3]{0:T(128)}, f32[3]{0:T(128)S(1)}, u32[]{:S(2)}) copy-start(f32[3]{0:T(128)S(1)} %compare_convert_fusion) | copy-start | bytes 40
  10.1 8.1 %collective-permute-start.4 = (f32[2,2,3]{2,0,1:T(2,128)S(1)}, f32[2,2,3]{2,0,1:T(2,128)S(1)}, u32[]{:S(2)}, u32[]{:S(2)}) collective-permute-start(f32[2,2,3]{2,0,1:T(2,128)S(1)} %broadcast_in_dim.221), channel_id=1, source_target_pairs={{0,224},{32,0},{64,32},{96,64},{128,96},{160,128},{192,160},{224,1... | collective-permute-start | bytes 152 | tf_op jit(solution)/shard_map/ppermute | solution.py:17
  19.3 4.2 collective-permute-start.5
  25.1 5.0 copy-start.19
  25.4 1.9 copy-start.12
  27.4 8.1 %collective-permute-start.3 = (f32[3,40,4,32]{3,2,1,0:T(4,128)S(1)}, f32[3,40,4,32]{3,2,1,0:T(4,128)S(1)}, u32[]{:S(2)}, u32[]{:S(2)}) collective-permute-start(f32[3,40,4,32]{3,2,1,0:T(4,128)S(1)} %get-tuple-element.368), channel_id=1, source_target_pairs={{1,0},{2,1},{3,2},{4,3},{5,4},{6,5},{7,6},{8,7},{9,8},{10,9},{11,1... | collective-permute-start | bytes 184328 | tf_op jit(solution)/shard_map/ppermute | solution.py:29
  30.1 7.4 %collective-permute-start.2 = (f32[3,40,4,32]{3,2,1,0:T(4,128)S(1)}, f32[3,40,4,32]{3,2,1,0:T(4,128)S(1)}, u32[]{:S(2)}, u32[]{:S(2)}) collective-permute-start(f32[3,40,4,32]{3,2,1,0:T(4,128)S(1)} %get-tuple-element.367), channel_id=1, source_target_pairs={{0,1},{1,2},{2,3},{3,4},{4,5},{5,6},{6,7},{7,8},{8,9},{9,10},{10,1... | collective-permute-start | bytes 184328 | tf_op jit(solution)/shard_map/ppermute | solution.py:27
  39.6 4.5 copy-start.20
  53.6 0.6 copy-start.8
  53.6 0.7 copy-start.10
  54.4 2.3 copy-start
  58.1 1.2 copy-start.7
  64.4 1.6 copy-start.5
  66.0 3.0 copy-start.3
  71.2 1.6 copy-start.6
  72.7 1.6 copy-start.1
  72.7 2.2 copy-start.2
  76.2 1.0 copy-start.4
  125.1 4.6 copy-start.9
  125.1 4.6 copy-start.11
  183.9 2.2 copy-start.13
  185.7 2.6 copy-start.16
  186.1 3.2 copy-start.21
  186.1 2.6 copy-start.14
  188.7 0.6 copy-start.17
  198.9 0.6 copy-start.8
  198.9 0.7 copy-start.10
  199.8 2.3 copy-start
  203.5 1.2 copy-start.7
  209.7 1.6 copy-start.5
  211.4 3.0 copy-start.3
  216.5 1.6 copy-start.6
  218.1 1.6 copy-start.1
  218.1 2.2 copy-start.2
  221.6 1.0 copy-start.4
  270.3 4.6 copy-start.9
  270.3 4.6 copy-start.11
  329.3 2.2 copy-start.13
  331.1 2.6 copy-start.16
  331.5 3.2 copy-start.21
  331.5 2.6 copy-start.14
  334.1 0.6 copy-start.17
  344.0 7.2 %collective-permute-start.6 = (f32[2,2,3]{2,1,0:T(2,128)S(1)}, f32[2,2,3]{2,1,0:T(2,128)S(1)}, u32[]{:S(2)}, u32[]{:S(2)}) collective-permute-start(f32[2,2,3]{2,1,0:T(2,128)S(1)} %pad_maximum_fusion.19), channel_id=1, source_target_pairs={{0,1},{1,2},{2,3},{3,4},{4,5},{5,6},{6,7},{7,8},{8,9},{9,10},{10,1... | collective-permute-start | bytes 152 | tf_op jit(solution)/shard_map/ppermute | solution.py:17
  351.3 4.6 collective-permute-start.7
  356.7 2.4 collective-permute-start.8
  359.1 8.2 %collective-permute-start.9 = (f32[2,2,3]{2,1,0:T(2,128)S(1)}, f32[2,2,3]{2,1,0:T(2,128)S(1)}, u32[]{:S(2)}, u32[]{:S(2)}) collective-permute-start(f32[2,2,3]{2,1,0:T(2,128)S(1)} %pad_maximum_fusion.20), channel_id=1, source_target_pairs={{0,31},{1,0},{2,1},{3,2},{4,3},{5,4},{6,5},{7,6},{8,7},{9,8},{10,9... | collective-permute-start | bytes 152 | tf_op jit(solution)/shard_map/ppermute | solution.py:17
  369.3 1.2 collective-permute-start.10
  370.6 4.2 collective-permute-start.11
  527.9 2.7 collective-permute-start.12
  530.6 3.9 collective-permute-start.13
  536.4 1.2 collective-permute-start.14
  537.7 4.2 collective-permute-start.15
  621.3 2.4 collective-permute-start.16
  623.7 3.7 collective-permute-start.17
  631.4 1.8 copy-start.15
